TPU v7x, 32 devices: a whole 2x2x4 slice. The times are simulated.
32 devices in a mesh: blk: 4 (over z), virt: 8 (over y, x, core).
Axes of the slice: x: 2, y: 2, z: 4, core: 2. Of those that a mesh axis runs over, the one named last changes fastest.
Arguments:
- integrals: bfloat16 [512, 16, 4096], P(('blk', 'virt')), may hold values from -0.09375 to 0.09375
- amplitudes: bfloat16 [256, 4096], P('blk'), may hold values from -6 to 6
- readers: int32 [512], P(('blk', 'virt')), may hold values from 0 to 7, as said below
- row_slots: int32 [512], P(('blk', 'virt')), may hold values from 0 to 3
- tile_mask: int32 [512, 4], P(('blk', 'virt')), may hold values 0 or 1
- virt_energy: float32 [2048], P(('blk', 'virt')), may hold values from 1 to 3
- occ_energy: float32 [1200], replicated, may hold values from -1 to -0.25
- pair_first: int32 [256], replicated, may hold values from 0 to 1199
- pair_second: int32 [256], replicated, may hold values from 0 to 1199
Outputs:
- update: bfloat16 [2048, 256], P(('blk', 'virt'))
Inputs may be any that keep to these rules, and one draw needn't show every extreme that they name: `readers`: each tile names a reader on the virt axis in the same blk row as its generating device; one device names one reader at most 4 times, and in every blk row some reader is named 4 times by every device of that row.
All inputs are finite; a program needn't handle non-finite values. No bound on the sum of `tile_mask` on one device may be relied on, other than what follows from the above.
Results may differ from a plain program's by a relative error of at most 0.001.
Values may be sent and summed in bfloat16 or wider, within the bound.
A program may use at most 64 MiB of HBM per device.

v0:
```python
import jax
import jax.numpy as jnp
from jax import lax
from jax.sharding import PartitionSpec as P


def body(
    integrals,
    amplitudes,
    readers,
    row_slots,
    tile_mask,
    virt_energy,
    occ_energy,
    pair_first,
    pair_second,
):
    virt_count = lax.axis_size("virt")
    blk_count = lax.axis_size("blk")
    generated = integrals.shape[0]
    tile_rows = integrals.shape[1]
    panel_rows = amplitudes.shape[0]
    capacity = max(1, 2 * generated // virt_count)
    slot_count = virt_count * capacity
    row_blocks = virt_energy.shape[0] // tile_rows
    tile_order = jnp.arange(generated, dtype=jnp.int32)
    same_reader = readers[:, None] == readers[None, :]
    earlier = tile_order[None, :] < tile_order[:, None]
    within = jnp.sum((same_reader & earlier).astype(jnp.int32), axis=1)
    position = readers * capacity + within
    placing = jnp.arange(slot_count, dtype=jnp.int32)[:, None] == position[None, :]
    filled = jnp.any(placing, axis=1)
    source_tile = jnp.sum(placing.astype(jnp.int32) * tile_order[None, :], axis=1)
    row_hot = (row_slots[:, None] == jnp.arange(row_blocks, dtype=jnp.int32)[None, :]).astype(
        jnp.float32
    )
    mask_float = tile_mask.astype(jnp.float32)
    sent_tiles = jnp.where(
        filled[:, None, None], integrals[source_tile], jnp.zeros((), jnp.bfloat16)
    )
    coefficient = (row_hot[:, :, None] * mask_float[:, None, :]).reshape(
        generated, row_blocks * blk_count
    )
    sent_coef = jnp.where(filled[:, None], coefficient[source_tile], 0.0).astype(jnp.bfloat16)
    got_tiles, got_coef = (
        lax.all_to_all(sent_tiles, "virt", split_axis=0, concat_axis=0, tiled=True),
        lax.all_to_all(sent_coef, "virt", split_axis=0, concat_axis=0, tiled=True),
    )
    got_coef = got_coef.astype(jnp.float32).reshape(slot_count, row_blocks, blk_count)
    panel = lax.all_gather(amplitudes, "blk", axis=0, tiled=True)
    column_count = panel.shape[0]
    column_panel = jnp.arange(column_count, dtype=jnp.int32) // panel_rows
    columns = jnp.einsum(
        "srk,kp->srp",
        got_coef,
        (jnp.arange(blk_count, dtype=jnp.int32)[:, None] == column_panel[None, :]).astype(
            jnp.float32
        ),
        precision=lax.Precision.HIGHEST,
    )
    product = jnp.einsum("stw,pw->stp", got_tiles, panel, preferred_element_type=jnp.float32)
    summed_panel = jnp.einsum("srp,stp->rtp", columns, product, precision=lax.Precision.HIGHEST)
    summed = summed_panel.reshape(row_blocks * tile_rows, column_count)
    levels = jnp.arange(occ_energy.shape[0], dtype=jnp.int32)[None, :]
    first_energy = jnp.sum(
        jnp.where(pair_first[:, None] == levels, occ_energy[None, :], 0.0), axis=1
    )
    second_energy = jnp.sum(
        jnp.where(pair_second[:, None] == levels, occ_energy[None, :], 0.0), axis=1
    )
    denominator = virt_energy[:, None] - first_energy[None, :] - second_energy[None, :]
    return (summed / denominator).astype(jnp.bfloat16)


def solution(mesh):
    placed = (
        P(("blk", "virt"), None, None),
        P("blk", None),
        P(("blk", "virt")),
        P(("blk", "virt")),
        P(("blk", "virt"), None),
        P(("blk", "virt")),
        P(),
        P(),
        P(),
    )
    return jax.shard_map(
        body, mesh=mesh, in_specs=placed, out_specs=P(("blk", "virt"), None), check_vma=False
    )
```

profile of v0, /device:TPU:0, one launch (start us, length us, event | category | flops | bytes accessed | tf_op | source)
XLA Modules:
  0.0 97.9 jit_solution(15406979760878977125)
XLA Ops:
  6.5 0.0 copy-start
  6.5 1.0 %convert_reduce_fusion = s32[16]{0:T(128)S(1)} fusion(s32[16]{0:T(128)} %param.11), kind=kLoop, calls=%fused_computation.16 | loop fusion | flops 1264 | bytes 128 | tf_op jit(solution)/shard_map/reduce_sum | solution.py:29
  7.5 0.7 multiply_add_fusion
  8.2 0.1 select_reduce_fusion.2
  8.3 0.1 fusion.5
  8.4 0.7 convert_element_type.25
  9.1 0.7 fusion.10
  9.8 0.1 copy.20
  9.8 0.1 broadcast_in_dim.44
  9.9 0.6 gather_fusion.1
  10.5 0.7 select_convert_fusion
  11.2 5.2 %all-to-all-start.1 = ((bf16[8,4,16]{2,1,0:T(4,128)(2,1)}), bf16[8,4,16]{2,1,0:T(4,128)(2,1)S(1)}, u32[]{:S(2)}, u32[]{:S(2)}) async-start(bf16[8,4,16]{2,1,0:T(4,128)(2,1)} %select_convert_fusion), calls=%async_computation.1 | async-start | bytes 16384 | tf_op jit(solution)/shard_map/all_to_all | solution.py:47
  16.4 0.0 copy-done
  16.4 2.8 %gather_fusion = bf16[32,16,4096]{2,1,0:T(8,128)(2,1)} fusion(bf16[16,16,4096]{2,1,0:T(8,128)(2,1)S(1)} %copy-done, s32[1024]{0:T(1024)S(1)} %pad_clamp_fusion), kind=kCustom, calls=%fused_computation | custom fusion | bytes 8388736 | tf_op jit(solution)/shard_map/gather | solution.py:39
  19.2 4.5 %broadcast_select_fusion = bf16[32,16,4096]{2,1,0:T(8,128)(2,1)} fusion(bf16[32,16,4096]{2,1,0:T(8,128)(2,1)} %gather_fusion, pred[32]{0:T(512)(128)(4,1)S(1)} %fusion.5), kind=kLoop, calls=%fused_computation.2 | loop fusion | flops 2097152 | bytes 8388640 | tf_op jit(solution)/shard_map/jit(_where)/select_n | solution.py:38
  23.7 0.0 all-to-all-done.1
  23.7 4.7 %all-to-all-start = ((bf16[32,16,4096]{2,1,0:T(8,128)(2,1)}), bf16[32,16,4096]{2,1,0:T(8,128)(2,1)}, u32[]{:S(2)}, u32[]{:S(2)}) async-start(bf16[32,16,4096]{2,1,0:T(8,128)(2,1)} %broadcast_select_fusion), calls=%async_computation | async-start | bytes 8388608 | tf_op jit(solution)/shard_map/all_to_all | solution.py:46
  28.4 0.0 all-gather.2.cloned.1.call-start
  28.4 0.7 all-gather.2.cloned.1.call-update
  29.1 0.0 copy-done.1
  29.1 0.0 copy-done.2
  29.2 0.4 select_reduce_fusion.1
  29.5 0.1 reshape.99
  29.6 0.1 fusion.3
  29.8 0.2 copy.23
  30.0 48.4 %all-gather.2.cloned.1.call-done = bf16[256,4096]{1,0:T(8,128)(2,1)} async-done(((bf16[64,4096]{1,0:T(8,128)(2,1)}), bf16[256,4096]{1,0:T(8,128)(2,1)}) %all-gather.2.cloned.1.call-update) | async-done | bytes 2097168 | tf_op jit(solution)/shard_map/all_gather | solution.py:50
  78.4 0.0 all-to-all-done
  78.4 4.1 %fusion = f32[32,16,256]{2,1,0:T(8,128)S(1)} fusion(bf16[32,16,4096]{2,1,0:T(8,128)(2,1)} %all-to-all-done, bf16[256,4096]{1,0:T(8,128)(2,1)} %all-gather.2.cloned.1.call-done), kind=kOutput, calls=%fused_computation.3 | convolution fusion | flops 1073741824 | bytes 6815744 | tf_op jit(solution)/shard_map/stw,pw->stp/dot_general | solution.py:61
  82.6 2.6 %copy.22 = f32[32,16,256]{0,1,2:T(8,128)} copy(f32[32,16,256]{2,1,0:T(8,128)S(1)} %fusion) | data formatting | bytes 1048576 | tf_op jit(solution)/shard_map/stw,pw->stp/dot_general | solution.py:61
  85.2 5.0 %convolution_bitcast_fusion = f32[4,16,256]{1,0,2:T(4,128)S(1)} fusion(f32[32,16,256]{0,1,2:T(8,128)} %copy.22, f32[32,4,256]{0,1,2:T(4,128)S(1)} %copy.23), kind=kOutput, calls=%fused_computation.5 | convolution fusion | flops 6291456 | bytes 720896 | tf_op jit(solution)/shard_map/srp,stp->rtp/dot_general | solution.py:62
  90.2 0.2 copy.24
  90.4 0.7 fusion.2
  (10 shorter events, 0.0 us)
Async XLA Ops:
  6.5 9.8 %copy-start = (bf16[16,16,4096]{2,1,0:T(8,128)(2,1)S(1)}, bf16[16,16,4096]{2,1,0:T(8,128)(2,1)}, u32[]{:S(2)}) copy-start(bf16[16,16,4096]{2,1,0:T(8,128)(2,1)} %param.9) | copy-start | bytes 6291460
  11.2 12.5 %all-to-all-start.1 = ((bf16[8,4,16]{2,1,0:T(4,128)(2,1)}), bf16[8,4,16]{2,1,0:T(4,128)(2,1)S(1)}, u32[]{:S(2)}, u32[]{:S(2)}) async-start(bf16[8,4,16]{2,1,0:T(4,128)(2,1)} %select_convert_fusion), calls=%async_computation.1 | async-start | bytes 16384 | tf_op jit(solution)/shard_map/all_to_all | solution.py:47
  23.7 5.5 %copy-start.1 = (f32[1200]{0:T(1024)S(1)}, f32[1200]{0:T(1024)}, u32[]{:S(2)}) copy-start(f32[1200]{0:T(1024)} %param.15) | copy-start | bytes 14404
  23.7 5.5 %copy-start.2 = (s32[256]{0:T(256)S(1)}, s32[256]{0:T(256)}, u32[]{:S(2)}) copy-start(s32[256]{0:T(256)} %param.16) | copy-start | bytes 3076
  23.7 5.5 %copy-start.3 = (s32[256]{0:T(256)S(1)}, s32[256]{0:T(256)}, u32[]{:S(2)}) copy-start(s32[256]{0:T(256)} %param.17) | copy-start | bytes 3076
  23.7 54.8 %all-to-all-start = ((bf16[32,16,4096]{2,1,0:T(8,128)(2,1)}), bf16[32,16,4096]{2,1,0:T(8,128)(2,1)}, u32[]{:S(2)}, u32[]{:S(2)}) async-start(bf16[32,16,4096]{2,1,0:T(8,128)(2,1)} %broadcast_select_fusion), calls=%async_computation | async-start | bytes 8388608 | tf_op jit(solution)/shard_map/all_to_all | solution.py:46
  28.4 50.1 %all-gather.2.cloned.1.call-start = ((), (), s32[]{:S(2)}) async-start(), calls=%async_computation.2 | async-start | bytes 2621440 | tf_op jit(solution)/shard_map/all_gather | solution.py:50
  85.2 5.2 %copy-start.4 = (f32[64]{0:T(128)S(1)}, f32[64]{0:T(128)}, u32[]{:S(2)}) copy-start(f32[64]{0:T(128)} %param.14) | copy-start | bytes 772
Sparse Core Ops, SparseCore 0:
  30.8 47.6 all-gather.1
where the time goes:
time: 98.4 us; the launch traced here: 97.9 us
  waiting for transfers between devices  49.1 us (50%)
  between operations  13.5 us (14%)
  starting transfers between devices  9.9 us (10%)
  other arithmetic  9.47 us (10%)
  matrix products  9.28 us (9%)
  local copies, waits for them, and re-layouts  6.7 us (7%)
    all_gather x1, waiting for transfers between devices, body(): panel = lax.all_gather(amplitudes, 'blk', axis=0, tiled=True)  48.4 us
    all_to_all x1, starting transfers between devices, body(): lax.all_to_all(sent_coef, 'virt', split_axis=0, concat_axis=0, tiled=True)  5.17 us
    dot_general x1, matrix products, body(): jnp.einsum('srp,stp->rtp', columns, product, precision=lax.Precision.HIGH...  4.99 us
    all_to_all x1, starting transfers between devices, body(): lax.all_to_all(sent_tiles, 'virt', split_axis=0, concat_axis=0, tiled=True)  4.69 us
    select_n x1, other arithmetic, body(): jnp.where(filled[:, None, None], integrals[source_tile], jnp.zeros((), jn...  4.5 us
    dot_general x1, matrix products, body(): jnp.einsum('stw,pw->stp', got_tiles, panel, preferred_element_type=jnp.fl...  4.15 us
    gather x1, local copies, waits for them, and re-layouts, body(): integrals[source_tile]  2.79 us
    dot_general x1, local copies, waits for them, and re-layouts, body(): jnp.einsum('stw,pw->stp', got_tiles, panel, preferred_element_type=jnp.fl...  2.62 us
  transfers between devices with their start and end apart: 3, of which 1 were waited for; matrix products, arithmetic and copies ran while one was open for 8% of the time, Pallas kernels for 0%

commit v1 on v0

--- a/solution.py
+++ b/solution.py
@@ -2,6 +2,28 @@
 import jax.numpy as jnp
 from jax import lax
 from jax.sharding import PartitionSpec as P
+
+
+def in_order(tiles, dim):
+    dims = list(tiles.shape[1:])
+    dims[dim] *= tiles.shape[0]
+    return jnp.moveaxis(tiles, 0, dim).reshape(dims)
+
+
+def collected_by_bits(x, axis):
+    devices = lax.axis_size(axis)
+    tiles = x[None]
+    for level in range(devices.bit_length() - 1):
+        bit = 1 << level
+        theirs = lax.ppermute(tiles, axis, [(i, i ^ bit) for i in range(devices)])
+        both = jnp.stack([tiles, theirs])
+        upper = lax.axis_index(axis) >> level & 1
+        tiles = jnp.where(upper == 0, both, both[::-1]).reshape(-1, *x.shape)
+    return tiles
+
+
+def gather_by_bits(value, axis, dim):
+    return in_order(collected_by_bits(value, axis), dim)
 
 
 def body(
@@ -47,7 +69,7 @@
         lax.all_to_all(sent_coef, "virt", split_axis=0, concat_axis=0, tiled=True),
     )
     got_coef = got_coef.astype(jnp.float32).reshape(slot_count, row_blocks, blk_count)
-    panel = lax.all_gather(amplitudes, "blk", axis=0, tiled=True)
+    panel = gather_by_bits(amplitudes, "blk", 0)
     column_count = panel.shape[0]
     column_panel = jnp.arange(column_count, dtype=jnp.int32) // panel_rows
     columns = jnp.einsum(

time: 98.4 us -> 90.4 us (0.919)
  between operations: 13.5 us -> 0.11 us
  other arithmetic: 9.47 us -> 14.1 us
  waiting for transfers between devices: 49.1 us -> 45 us
  starting transfers between devices: 9.9 us -> 14 us
    all_gather x1 -> x0, waiting for transfers between devices: 48.4 us -> none  [body(): panel = lax.all_gather(amplitudes, 'blk', axis=0, tiled=True)]
    ppermute x0 -> x2, waiting for transfers between devices: none -> 45 us  [collected_by_bits(): theirs = lax.ppermute(tiles, axis, [(i, i ^ bit) for i in range(devices)])]
    ppermute x0 -> x2, starting transfers between devices: none -> 5.61 us  [collected_by_bits(): theirs = lax.ppermute(tiles, axis, [(i, i ^ bit) for i in range(devices)])]
    another operation x0 -> x3, other arithmetic: none -> 2.88 us  [collected_by_bits(): both = jnp.stack([tiles, theirs])]
    select_n x0 -> x1, other arithmetic: none -> 1.87 us  [collected_by_bits(): tiles = jnp.where(upper == 0, both, both[::-1]).reshape(-1, *x.shape)]
    all_to_all x1, starting transfers between devices: 5.17 us -> 3.72 us  [body(): lax.all_to_all(sent_coef, 'virt', split_axis=0, concat_axis=0, tiled=True)]
  transfers between devices with their start and end apart: 3 -> 4, of which waited for: 1 -> 1; matrix products, arithmetic and copies ran while one was open for 8% -> 20% of each run, Pallas kernels for 0% -> 0%
where the time goes in v1:
time: 90.4 us; the launch traced here: 90 us
  waiting for transfers between devices  45 us (50%)
  other arithmetic  14.1 us (16%)
  starting transfers between devices  14 us (15%)
  matrix products  9.29 us (10%)
  local copies, waits for them, and re-layouts  7.51 us (8%)
    ppermute x2, waiting for transfers between devices, collected_by_bits(): theirs = lax.ppermute(tiles, axis, [(i, i ^ bit) for i in range(devices)])  45 us
    ppermute x2, starting transfers between devices, collected_by_bits(): theirs = lax.ppermute(tiles, axis, [(i, i ^ bit) for i in range(devices)])  5.61 us
    dot_general x1, matrix products, body(): jnp.einsum('srp,stp->rtp', columns, product, precision=lax.Precision.HIGH...  4.99 us
    all_to_all x1, starting transfers between devices, body(): lax.all_to_all(sent_tiles, 'virt', split_axis=0, concat_axis=0, tiled=True)  4.67 us
    select_n x1, other arithmetic, body(): jnp.where(filled[:, None, None], integrals[source_tile], jnp.zeros((), jn...  4.49 us
    dot_general x1, matrix products, body(): jnp.einsum('stw,pw->stp', got_tiles, panel, preferred_element_type=jnp.fl...  4.15 us
    all_to_all x1, starting transfers between devices, body(): lax.all_to_all(sent_coef, 'virt', split_axis=0, concat_axis=0, tiled=True)  3.72 us
    another operation x3, other arithmetic, collected_by_bits(): both = jnp.stack([tiles, theirs])  2.88 us
  transfers between devices with their start and end apart: 4, of which 1 were waited for; matrix products, arithmetic and copies ran while one was open for 20% of the time, Pallas kernels for 0%

profile of v1, /device:TPU:0, one launch (start us, length us, event | category | flops | bytes accessed | tf_op | source)
XLA Modules:
  0.0 90.0 jit_solution(11145431066976472556)
XLA Ops:
  0.0 3.0 %collective-permute-start = (bf16[1,64,4096]{2,1,0:T(8,128)(2,1)}, bf16[1,64,4096]{2,1,0:T(8,128)(2,1)S(1)}, u32[]{:S(2)}, u32[]{:S(2)}) collective-permute-start(bf16[1,64,4096]{2,1,0:T(8,128)(2,1)} %bitcast.31), channel_id=1, source_target_pairs={{0,8},{8,0},{16,24},{24,16},{1,9},{9,1},{17,25},{25,17},{2,10},{10... | collective-permute-start | bytes 1572872 | tf_op jit(solution)/shard_map/ppermute | solution.py:18
  3.0 0.9 %convert_reduce_fusion = s32[16]{0:T(128)S(1)} fusion(s32[16]{0:T(128)} %param.11), kind=kLoop, calls=%fused_computation.20 | loop fusion | flops 1264 | bytes 128 | tf_op jit(solution)/shard_map/reduce_sum | solution.py:51
  3.9 0.7 multiply_add_fusion
  4.6 0.1 select_reduce_fusion.2
  4.7 0.1 fusion.5
  4.8 0.7 convert_element_type.25
  5.5 0.7 fusion.10
  6.2 0.1 copy.20
  6.2 0.1 broadcast_in_dim.47
  6.3 0.6 gather_fusion.1
  6.9 0.7 select_convert_fusion
  7.6 3.7 %all-to-all-start.1 = ((bf16[8,4,16]{2,1,0:T(4,128)(2,1)}), bf16[8,4,16]{2,1,0:T(4,128)(2,1)S(1)}, u32[]{:S(2)}, u32[]{:S(2)}) async-start(bf16[8,4,16]{2,1,0:T(4,128)(2,1)} %select_convert_fusion), calls=%async_computation.1 | async-start | bytes 16384 | tf_op jit(solution)/shard_map/all_to_all | solution.py:69
  11.3 2.8 %gather_fusion = bf16[32,16,4096]{2,1,0:T(8,128)(2,1)} fusion(bf16[16,16,4096]{2,1,0:T(8,128)(2,1)S(1)} %copy-done, s32[1024]{0:T(1024)S(1)} %pad_clamp_fusion), kind=kCustom, calls=%fused_computation | custom fusion | bytes 8388736 | tf_op jit(solution)/shard_map/gather | solution.py:61
  14.1 4.5 %broadcast_select_fusion = bf16[32,16,4096]{2,1,0:T(8,128)(2,1)} fusion(bf16[32,16,4096]{2,1,0:T(8,128)(2,1)} %gather_fusion, pred[32]{0:T(512)(128)(4,1)S(1)} %fusion.5), kind=kLoop, calls=%fused_computation.2 | loop fusion | flops 2097152 | bytes 8388640 | tf_op jit(solution)/shard_map/jit(_where)/select_n | solution.py:60
  18.6 4.7 %all-to-all-start = ((bf16[32,16,4096]{2,1,0:T(8,128)(2,1)}), bf16[32,16,4096]{2,1,0:T(8,128)(2,1)}, u32[]{:S(2)}, u32[]{:S(2)}) async-start(bf16[32,16,4096]{2,1,0:T(8,128)(2,1)} %broadcast_select_fusion), calls=%async_computation | async-start | bytes 8388608 | tf_op jit(solution)/shard_map/all_to_all | solution.py:68
  23.3 0.1 pad_maximum_fusion.1
  23.4 0.0 copy-start.3
  23.4 0.0 copy-start.4
  23.5 1.4 %fusion.1 = (bf16[1,2,64,4096]{3,2,1,0:T(8,128)(2,1)S(1)}, bf16[2,64,4096]{2,1,0:T(8,128)(2,1)}) fusion(bf16[2,1,64,4096]{3,2,1,0:T(8,128)(2,1)S(1)} %pad_maximum_fusion.1, pred[]{:T(512)S(6)} %eq.95), kind=kLoop, calls=%fused_computation.13 | loop fusion | flops 524288 | bytes 3145729 | tf_op jit(solution)/shard_map/stack;reshape | solution.py:19
  24.8 2.6 %collective-permute-start.1 = (bf16[2,64,4096]{2,1,0:T(8,128)(2,1)}, bf16[2,64,4096]{2,1,0:T(8,128)(2,1)}, u32[]{:S(2)}, u32[]{:S(2)}) collective-permute-start(bf16[2,64,4096]{2,1,0:T(8,128)(2,1)} %get-tuple-element.8), channel_id=1, source_target_pairs={{0,16},{8,24},{16,0},{24,8},{1,17},{9,25},{17,1},{25,9},{2,18},{10... | collective-permute-start | bytes 3145736 | tf_op jit(solution)/shard_map/ppermute | solution.py:18
  27.4 0.4 select_reduce_fusion.1
  27.8 0.1 reshape.103
  27.9 0.1 fusion.3
  28.0 1.0 %copy.23 = f32[32,4,256]{0,1,2:T(4,128)} copy(f32[32,4,256]{2,0,1:T(8,128)S(1)} %fusion.3) | data formatting | bytes 262144 | tf_op jit(solution)/shard_map/srk,kp->srp/dot_general | solution.py:75
  29.1 45.0 %collective-permute-done.1 = bf16[2,64,4096]{2,1,0:T(8,128)(2,1)} collective-permute-done((bf16[2,64,4096]{2,1,0:T(8,128)(2,1)}, bf16[2,64,4096]{2,1,0:T(8,128)(2,1)}, u32[]{:S(2)}, u32[]{:S(2)}) %collective-permute-start.1) | collective-permute-done | bytes 1048608 | tf_op jit(solution)/shard_map/ppermute | solution.py:18
  74.1 1.4 %pad_maximum_fusion = bf16[2,2,64,4096]{3,2,1,0:T(8,128)(2,1)S(1)} fusion(bf16[1,2,64,4096]{3,2,1,0:T(8,128)(2,1)} %bitcast.7, bf16[1,2,64,4096]{3,2,1,0:T(8,128)(2,1)S(1)} %get-tuple-element.7), kind=kLoop, calls=%fused_computation.4 | loop fusion | flops 1048576 | bytes 4194304 | tf_op jit(solution)/shard_map/stack | solution.py:19
  75.5 1.9 %reverse_select_fusion = bf16[2,2,64,4096]{3,2,1,0:T(8,128)(2,1)} fusion(bf16[2,2,64,4096]{3,2,1,0:T(8,128)(2,1)S(1)} %pad_maximum_fusion, pred[]{:T(512)S(6)} %eq.94), kind=kLoop, calls=%fused_computation.3 | loop fusion | flops 1048576 | bytes 4194305 | tf_op jit(solution)/shard_map/jit(_where)/select_n | solution.py:21
  77.3 4.2 %fusion.12 = f32[32,16,256]{2,1,0:T(8,128)S(1)} fusion(bf16[32,16,4096]{2,1,0:T(8,128)(2,1)} %all-to-all-done, bf16[256,4096,1]{1,0,2:T(8,128)(2,1)} %bitcast.30), kind=kOutput, calls=%fused_computation.39 | convolution fusion | flops 1073741824 | bytes 6815744 | tf_op jit(solution)/shard_map/stw,pw->stp/dot_general | solution.py:83
  81.5 2.6 %copy.22 = f32[32,16,256]{0,1,2:T(8,128)} copy(f32[32,16,256]{2,1,0:T(8,128)S(1)} %fusion.12) | data formatting | bytes 1048576 | tf_op jit(solution)/shard_map/stw,pw->stp/dot_general | solution.py:83
  84.1 5.0 %convolution_bitcast_fusion = f32[4,16,256]{1,0,2:T(4,128)S(1)} fusion(f32[32,16,256]{0,1,2:T(8,128)} %copy.22, f32[32,4,256]{0,1,2:T(4,128)S(1)} %copy-done.1), kind=kOutput, calls=%fused_computation.6 | convolution fusion | flops 6291456 | bytes 720896 | tf_op jit(solution)/shard_map/srp,stp->rtp/dot_general | solution.py:84
  89.1 0.2 copy.24
  89.3 0.7 fusion.2
  (19 shorter events, 0.1 us)
Async XLA Ops:
  0.0 11.3 %copy-start = (bf16[16,16,4096]{2,1,0:T(8,128)(2,1)S(1)}, bf16[16,16,4096]{2,1,0:T(8,128)(2,1)}, u32[]{:S(2)}) copy-start(bf16[16,16,4096]{2,1,0:T(8,128)(2,1)} %param.9) | copy-start | bytes 6291460
  0.0 23.3 %collective-permute-start = (bf16[1,64,4096]{2,1,0:T(8,128)(2,1)}, bf16[1,64,4096]{2,1,0:T(8,128)(2,1)S(1)}, u32[]{:S(2)}, u32[]{:S(2)}) collective-permute-start(bf16[1,64,4096]{2,1,0:T(8,128)(2,1)} %bitcast.31), channel_id=1, source_target_pairs={{0,8},{8,0},{16,24},{24,16},{1,9},{9,1},{17,25},{25,17},{2,10},{10... | collective-permute-start | bytes 1572872 | tf_op jit(solution)/shard_map/ppermute | solution.py:18
  7.6 11.0 %all-to-all-start.1 = ((bf16[8,4,16]{2,1,0:T(4,128)(2,1)}), bf16[8,4,16]{2,1,0:T(4,128)(2,1)S(1)}, u32[]{:S(2)}, u32[]{:S(2)}) async-start(bf16[8,4,16]{2,1,0:T(4,128)(2,1)} %select_convert_fusion), calls=%async_computation.1 | async-start | bytes 16384 | tf_op jit(solution)/shard_map/all_to_all | solution.py:69
  18.6 4.7 %copy-start.2 = (bf16[64,4096]{1,0:T(8,128)(2,1)S(1)}, bf16[64,4096]{1,0:T(8,128)(2,1)}, u32[]{:S(2)}) copy-start(bf16[64,4096]{1,0:T(8,128)(2,1)} %param.10) | copy-start | bytes 1572868
  18.6 58.7 %all-to-all-start = ((bf16[32,16,4096]{2,1,0:T(8,128)(2,1)}), bf16[32,16,4096]{2,1,0:T(8,128)(2,1)}, u32[]{:S(2)}, u32[]{:S(2)}) async-start(bf16[32,16,4096]{2,1,0:T(8,128)(2,1)} %broadcast_select_fusion), calls=%async_computation | async-start | bytes 8388608 | tf_op jit(solution)/shard_map/all_to_all | solution.py:68
  23.4 4.0 %copy-start.3 = (f32[1200]{0:T(1024)S(1)}, f32[1200]{0:T(1024)}, u32[]{:S(2)}) copy-start(f32[1200]{0:T(1024)} %param.15) | copy-start | bytes 14404
  23.4 4.0 %copy-start.4 = (s32[256]{0:T(256)S(1)}, s32[256]{0:T(256)}, u32[]{:S(2)}) copy-start(s32[256]{0:T(256)} %param.16) | copy-start | bytes 3076
  23.4 4.0 %copy-start.5 = (s32[256]{0:T(256)S(1)}, s32[256]{0:T(256)}, u32[]{:S(2)}) copy-start(s32[256]{0:T(256)} %param.17) | copy-start | bytes 3076
  24.8 49.2 %collective-permute-start.1 = (bf16[2,64,4096]{2,1,0:T(8,128)(2,1)}, bf16[2,64,4096]{2,1,0:T(8,128)(2,1)}, u32[]{:S(2)}, u32[]{:S(2)}) collective-permute-start(bf16[2,64,4096]{2,1,0:T(8,128)(2,1)} %get-tuple-element.8), channel_id=1, source_target_pairs={{0,16},{8,24},{16,0},{24,8},{1,17},{9,25},{17,1},{25,9},{2,18},{10... | collective-permute-start | bytes 3145736 | tf_op jit(solution)/shard_map/ppermute | solution.py:18
  81.5 2.6 %copy-start.1 = (f32[32,4,256]{0,1,2:T(4,128)S(1)}, f32[32,4,256]{0,1,2:T(4,128)}, u32[]{:S(2)}) copy-start(f32[32,4,256]{0,1,2:T(4,128)} %copy.23) | copy-start | bytes 393220
  84.1 5.2 %copy-start.6 = (f32[64]{0:T(128)S(1)}, f32[64]{0:T(128)}, u32[]{:S(2)}) copy-start(f32[64]{0:T(128)} %param.14) | copy-start | bytes 772
